TPU v7x, 32 devices: a whole 2x2x4 slice. The times are simulated.
32 devices in a mesh: dp: 8 (over y, x, core), tp: 4 (over z).
Axes of the slice: x: 2, y: 2, z: 4, core: 2. Of those that a mesh axis runs over, the one named last changes fastest.
Arguments:
- block_in: bfloat16 [128, 4, 37632], P('dp', 'tp'), may hold values from -6 to 6
- ln1_gain: float32 [768], P('tp'), may hold values from 0.1 to 1.9
- ln1_shift: float32 [768], P('tp'), may hold values from -1.75 to 1.75
- tok_w1: float32 [196, 384], replicated, may hold values from -0.4375 to 0.4375
- tok_b1: float32 [384], replicated, may hold values from -1.75 to 1.75
- tok_w2: float32 [384, 196], replicated, may hold values from -0.3125 to 0.3125
- tok_b2: float32 [196], replicated, may hold values from -1.75 to 1.75
- ln2_gain: float32 [768], P('tp'), may hold values from 0.1 to 1.9
- ln2_shift: float32 [768], P('tp'), may hold values from -1.75 to 1.75
- ch_w1: float32 [768, 3072], P('dp', 'tp'), may hold values from -0.21875 to 0.21875
- ch_b1: float32 [3072], replicated, may hold values from -1.75 to 1.75
- ch_w2: float32 [3072, 768], P('tp', 'dp'), may hold values from -0.109375 to 0.109375
- ch_b2: float32 [768], replicated, may hold values from -1.75 to 1.75
- group_ids: int32 [128], P('dp'), may hold values from 0 to 63
- out_grad: bfloat16 [128, 4, 37632], P('dp', 'tp'), may hold values from -6 to 6
Outputs:
- block_out: bfloat16 [128, 4, 37632], P('dp', 'tp')
- dx: bfloat16 [128, 4, 37632], P('dp', 'tp')
- group_norms: float32 [64], replicated
- d_ln1_gain: float32 [768], P('tp')
- d_ln1_shift: float32 [768], P('tp')
- d_tok_w1: float32 [196, 384], replicated
- d_tok_b1: float32 [384], replicated
- d_tok_w2: float32 [384, 196], replicated
- d_tok_b2: float32 [196], replicated
- d_ln2_gain: float32 [768], P('tp')
- d_ln2_shift: float32 [768], P('tp')
- d_ch_w1: float32 [768, 3072], P('dp', 'tp')
- d_ch_b1: float32 [3072], replicated
- d_ch_w2: float32 [3072, 768], P('tp', 'dp')
- d_ch_b2: float32 [768], replicated
All inputs are finite; a program needn't handle non-finite values.
Results may differ from a plain program's by a relative error of at most 0.01.
Values may be sent and summed in bfloat16 or wider, within the bound.
A program may use at most 128 MiB of HBM per device.

v0:
```python
import math
import jax
import jax.numpy as jnp
from jax import lax
from jax.sharding import PartitionSpec as P

S = 196
GROUPS = 64
epsilon = 1e-06
highest = lax.Precision.HIGHEST


def in_blocks(array, dim, size):
    lengths = array.shape
    tiles = array.reshape(*lengths[:dim], size, lengths[dim] // size, *lengths[dim + 1 :])
    return jnp.moveaxis(tiles, dim, 0)


def sum_at_owner(array, axis, dim):
    size = lax.axis_size(axis)
    tiles = lax.all_to_all(in_blocks(array, dim, size), axis, 0, 0, tiled=True)
    return jnp.sum(tiles.astype(jnp.float32), axis=0)


def norm_stats(values, full_width):
    totals = lax.psum((jnp.sum(values, -1), jnp.sum(values * values, -1)), "tp")
    average = totals[0] / full_width
    inverse = lax.rsqrt(totals[1] / full_width - average * average + epsilon)
    return ((values - average[..., None]) * inverse[..., None], inverse)


def norm_back(grad_hat, normed, inverse, full_width):
    totals = lax.psum((jnp.sum(grad_hat, -1), jnp.sum(grad_hat * normed, -1)), "tp")
    return inverse[..., None] * (
        grad_hat - totals[0][..., None] / full_width - normed * totals[1][..., None] / full_width
    )


def spread_slot(values, slot_mask):
    expanded = values[..., None, :] * slot_mask[:, None]
    return expanded.reshape(values.shape[:-1] + (slot_mask.shape[0] * values.shape[-1],))


def gather_channels(values):
    return lax.all_gather(values, "tp", axis=1, tiled=True)


def sum_channels(values):
    return lax.psum_scatter(
        values.astype(jnp.bfloat16), "tp", scatter_dimension=1, tiled=True
    ).astype(jnp.float32)


def per_device(
    block_in,
    ln1_gain,
    ln1_shift,
    tok_w1,
    tok_b1,
    tok_w2,
    tok_b2,
    ln2_gain,
    ln2_shift,
    ch_w1,
    ch_b1,
    ch_w2,
    ch_b2,
    group_ids,
    out_grad,
):
    f32 = jnp.float32
    bf16 = jnp.bfloat16
    images = block_in.shape[0]
    patches = S
    plain_in = block_in.reshape(images, patches, -1)
    plain_grad = out_grad.reshape(images, patches, -1)
    local_width = plain_in.shape[2]
    tp_count = lax.axis_size("tp")
    dp_count = lax.axis_size("dp")
    tp_place = lax.axis_index("tp")
    full_width = local_width * tp_count
    slot_mask = (jnp.arange(tp_count) == tp_place).astype(f32)
    row_count = images * patches
    input_float = plain_in.astype(f32)
    normed_one, inverse_one = norm_stats(input_float, full_width)
    mixed_in = (normed_one * ln1_gain + ln1_shift).astype(bf16)
    token_w1 = tok_w1.astype(bf16)
    token_w2 = tok_w2.astype(bf16)
    pre_act = jnp.einsum("nsc,sk->nck", mixed_in, token_w1, preferred_element_type=f32) + tok_b1
    hidden_act, gelu_token = jax.vjp(jax.nn.gelu, pre_act)
    hidden_low = hidden_act.astype(bf16)
    token_out = (
        jnp.einsum("nck,ks->nsc", hidden_low, token_w2, preferred_element_type=f32)
        + tok_b2[None, :, None]
    )
    residual = input_float + token_out
    normed_two, inverse_two = norm_stats(residual, full_width)
    branch_in = (normed_two * ln2_gain + ln2_shift).astype(bf16).reshape(row_count, local_width)
    grad_low = plain_grad.reshape(row_count, local_width)
    upper_rows, lower_rows = (
        lax.all_gather(ch_w1.astype(bf16), "dp", axis=0, tiled=True),
        lax.all_gather(ch_w2.astype(bf16), "dp", axis=1, tiled=True),
    )
    gathered = gather_channels(branch_in)
    hidden_width = upper_rows.shape[1]
    bias_first = lax.dynamic_slice_in_dim(ch_b1, tp_place * hidden_width, hidden_width)
    bias_second = lax.dynamic_slice_in_dim(ch_b2, tp_place * local_width, local_width)
    inner_act = jnp.dot(gathered, upper_rows, preferred_element_type=f32) + bias_first
    activated, gelu_branch = jax.vjp(jax.nn.gelu, inner_act)
    activated_low = activated.astype(bf16)
    branch_sum = (
        sum_channels(jnp.dot(activated_low, lower_rows, preferred_element_type=f32)) + bias_second
    )
    branch_low = branch_sum.astype(bf16)
    grad_full = gather_channels(grad_low)
    grad_activated = jnp.dot(grad_full, lower_rows.T, preferred_element_type=f32)
    grad_lower = jnp.dot(activated_low.T, grad_full, preferred_element_type=f32)
    grad_inner = gelu_branch(grad_activated)[0].astype(bf16)
    grad_upper = jnp.dot(gathered.T, grad_inner, preferred_element_type=f32)
    bias_first_grad = spread_slot(jnp.sum(grad_inner.astype(f32), 0), slot_mask)
    bias_second_grad = spread_slot(jnp.sum(grad_low.astype(f32), 0), slot_mask)
    grad_branch = sum_channels(jnp.dot(grad_inner, upper_rows.T, preferred_element_type=f32))
    upper_grad, lower_grad = (
        sum_at_owner(grad_upper.astype(jnp.bfloat16), "dp", 0),
        sum_at_owner(grad_lower.astype(jnp.bfloat16), "dp", 1),
    )
    output = (residual + branch_low.astype(f32).reshape(residual.shape)).astype(bf16)
    grad_normed = grad_branch.reshape(residual.shape)
    image_gain = jnp.sum(grad_normed * normed_two, 1)
    image_shift = jnp.sum(grad_normed, 1)
    grad_resid = plain_grad.astype(f32) + norm_back(
        grad_normed * ln2_gain, normed_two, inverse_two, full_width
    )
    grad_token_low = grad_resid.astype(bf16)
    grad_hidden = jnp.einsum("nsc,ks->nck", grad_token_low, token_w2, preferred_element_type=f32)
    token_w2_grad = jnp.einsum(
        "nck,nsc->ks", hidden_low, grad_token_low, preferred_element_type=f32
    )
    token_b2_grad = jnp.sum(grad_token_low.astype(f32), (0, 2))
    grad_pre = gelu_token(grad_hidden)[0].astype(bf16)
    token_w1_grad = jnp.einsum("nsc,nck->sk", mixed_in, grad_pre, preferred_element_type=f32)
    token_b1_grad = jnp.sum(grad_pre.astype(f32), (0, 1))
    grad_mixed = jnp.einsum("nck,sk->nsc", grad_pre, token_w1, preferred_element_type=f32)
    gain_one_grad = jnp.sum(grad_mixed * normed_one, (0, 1))
    shift_one_grad = jnp.sum(grad_mixed, (0, 1))
    grad_input = (
        grad_resid + norm_back(grad_mixed * ln1_gain, normed_one, inverse_one, full_width)
    ).astype(bf16)
    member = (group_ids[:, None] == jnp.arange(GROUPS)[None, :]).astype(f32)
    image_stats = jnp.stack([image_gain, image_shift], 1).reshape(images, 2 * local_width)
    group_local = jnp.dot(member.T, image_stats, precision=highest).reshape(GROUPS, 2, local_width)
    norm_one_local = jnp.stack([gain_one_grad, shift_one_grad], 0)
    totals = lax.psum(
        (
            token_w1_grad,
            token_b1_grad,
            token_w2_grad,
            token_b2_grad,
            spread_slot(group_local, slot_mask),
            spread_slot(norm_one_local, slot_mask),
            bias_first_grad,
            bias_second_grad,
        ),
        ("dp", "tp"),
    )
    group_full = totals[4]
    group_norms = jnp.sqrt(jnp.sum(group_full * group_full, (1, 2)))
    clip_bound = 2.0 * math.sqrt(images * dp_count * patches * full_width / GROUPS)
    factor = clip_bound / jnp.maximum(group_norms, clip_bound)
    clipped = jnp.sum(factor[:, None, None] * group_full, 0)
    clipped_local = lax.dynamic_slice_in_dim(clipped, tp_place * local_width, local_width, 1)
    norm_one_own = lax.dynamic_slice_in_dim(totals[5], tp_place * local_width, local_width, 1)
    stored_out = output.reshape(images, 1, patches * local_width)
    stored_grad = grad_input.reshape(images, 1, patches * local_width)
    return (
        stored_out,
        stored_grad,
        group_norms,
        norm_one_own[0],
        norm_one_own[1],
        totals[0],
        totals[1],
        totals[2],
        totals[3],
        clipped_local[0],
        clipped_local[1],
        upper_grad,
        totals[6],
        lower_grad,
        totals[7],
    )


def solution(mesh):
    in_specs = (
        P("dp", "tp", None),
        P("tp"),
        P("tp"),
        P(),
        P(),
        P(),
        P(),
        P("tp"),
        P("tp"),
        P("dp", "tp"),
        P(),
        P("tp", "dp"),
        P(),
        P("dp"),
        P("dp", "tp", None),
    )
    out_specs = (
        P("dp", "tp", None),
        P("dp", "tp", None),
        P(),
        P("tp"),
        P("tp"),
        P(),
        P(),
        P(),
        P(),
        P("tp"),
        P("tp"),
        P("dp", "tp"),
        P(),
        P("tp", "dp"),
        P(),
    )
    return jax.shard_map(
        per_device, mesh=mesh, in_specs=in_specs, out_specs=out_specs, check_vma=False
    )
```

profile of v0, /device:TPU:0, one launch (start us, length us, event | category | flops | bytes accessed | tf_op | source)
XLA Modules:
  0.0 688.9 jit_solution(15931302584527314932)
XLA Ops:
  7.2 1.6 convert_element_type.122
  8.9 2.2 reshape.136
  11.2 1.2 fusion.35
  12.3 3.2 copy.70
  15.6 20.9 %all-reduce.5 = (f32[16,196]{1,0:T(8,128)S(1)}, f32[16,196]{1,0:T(8,128)S(1)}) all-reduce(f32[16,196]{1,0:T(8,128)S(1)} %get-tuple-element.20, f32[16,196]{1,0:T(8,128)S(1)} %get-tuple-element.19), channel_id=1, replica_groups=mesh['dp'=8,'tp'=4] {'tp'}, use_global_device_ids=true, to_apply=%region_3.0 | all-reduce | flops 6272 | bytes 50176 | tf_op jit(solution)/shard_map/psum | solution.py:26
  36.5 2.5 add_convert_fusion.2
  39.0 1.1 copy-done.6
  40.2 1.0 fusion.22
  41.1 0.9 copy-done
  42.1 2.5 fusion.36
  44.6 15.8 %all-reduce.4 = (f32[16,196]{1,0:T(8,128)S(1)}, f32[16,196]{1,0:T(8,128)S(1)}) all-reduce(f32[16,196]{1,0:T(8,128)S(1)} %get-tuple-element.23, f32[16,196]{1,0:T(8,128)S(1)} %get-tuple-element.22), channel_id=1, replica_groups=mesh['dp'=8,'tp'=4] {'tp'}, use_global_device_ids=true, to_apply=%region_7.0 | all-reduce | flops 6272 | bytes 50176 | tf_op jit(solution)/shard_map/psum | solution.py:26
  60.5 1.3 add_convert_fusion.1
  61.7 2.0 copy.71
  63.8 4.3 reshape.126
  68.2 1.6 convert_element_type.124
  69.9 3.1 reshape_reshape.3
  72.9 2.0 copy.74
  75.2 0.8 dynamic_slice.12
  76.0 84.4 %all-gather.5.cloned.1.call-done = bf16[3136,768]{0,1:T(8,128)(2,1)} async-done(((bf16[3136,192]{0,1:T(8,128)(2,1)}), bf16[3136,768]{0,1:T(8,128)(2,1)}) %all-gather.5.cloned.1.call-update) | async-done | bytes 4816912 | tf_op jit(solution)/shard_map/all_gather | solution.py:45
  160.4 10.4 %fusion.40 = f32[3136,768]{1,0:T(8,128)} fusion(bf16[3136,768]{0,1:T(8,128)(2,1)} %all-gather.5.cloned.1.call-done, bf16[768,768]{1,0:T(8,128)(2,1)} %all-gather.7.cloned.1.call-done), kind=kOutput, calls=%fused_computation.92 | convolution fusion | flops 3699376128 | bytes 15630336 | tf_op jit(solution)/shard_map/dot_general | solution.py:108
  170.8 14.6 %all-gather.9.cloned.1.call-done = bf16[768,768]{0,1:T(8,128)(2,1)} async-done(((bf16[768,96]{0,1:T(8,128)(2,1)}), bf16[768,768]{0,1:T(8,128)(2,1)}) %all-gather.9.cloned.1.call-update) | async-done | bytes 1179664 | tf_op jit(solution)/shard_map/all_gather | solution.py:102
  185.4 10.6 %convolution_convert_fusion.1 = bf16[3136,768]{0,1:T(8,128)(2,1)} fusion(bf16[768,768]{0,1:T(8,128)(2,1)} %all-gather.9.cloned.1.call-done, f32[3136,768]{1,0:T(8,128)} %fusion.40, f32[768]{0:T(1024)S(1)} %dynamic_slice.12), kind=kOutput, calls=%fused_computation.14 | convolution fusion | flops 3725869056 | bytes 15633408 | tf_op jit(solution)/shard_map/dot_general | solution.py:112
  196.4 83.0 %all-gather.11.cloned.1.call-done = bf16[3136,768]{0,1:T(8,128)(2,1)} async-done(((bf16[3136,192]{0,1:T(8,128)(2,1)}), bf16[3136,768]{0,1:T(8,128)(2,1)}) %all-gather.11.cloned.1.call-update) | async-done | bytes 4816912 | tf_op jit(solution)/shard_map/all_gather | solution.py:45
  279.5 15.2 %convert_reduce_fusion = (f32[768]{0:T(1024)S(1)}, bf16[3136,768]{1,0:T(8,128)(2,1)S(1)}) fusion(f32[3136,768]{1,0:T(8,128)} %fusion.40, f32[768]{0:T(1024)S(1)} %dynamic_slice.12, bf16[3136,768]{0,1:T(8,128)(2,1)} %all-gather.11.cloned.1.call-done, bf16[768,768]{0,1:T(8,128)(2,1)} %all-gather.9.cloned.1.call-done), kind=kOutput, calls=%fused_computation.9 | convolution fusion | flops 3754769664 | bytes 20453376 | tf_op jit(solution)/shard_map/dot_general | solution.py:116
  294.7 2.1 copy-done.29
  296.8 5.9 convolution_convert_fusion
  302.7 10.6 %convolution_convert_fusion.2 = bf16[768,768]{0,1:T(8,128)(2,1)} fusion(bf16[3136,768]{0,1:T(8,128)(2,1)} %all-gather.11.cloned.1.call-done, f32[3136,768]{1,0:T(8,128)} %fusion.40, f32[768]{0:T(1024)S(1)} %dynamic_slice.12), kind=kOutput, calls=%fused_computation.49 | convolution fusion | flops 3724050432 | bytes 15633408 | tf_op jit(solution)/shard_map/dot_general | solution.py:117
  313.3 4.4 all-to-all-start.1
  317.8 9.1 %convolution_convert_fusion.3 = bf16[768,768]{1,0:T(8,128)(2,1)} fusion(bf16[3136,768]{0,1:T(8,128)(2,1)} %all-gather.5.cloned.1.call-done, bf16[3136,768]{1,0:T(8,128)(2,1)} %copy-done.29), kind=kOutput, calls=%fused_computation.50 | convolution fusion | flops 3699965952 | bytes 10813440 | tf_op jit(solution)/shard_map/dot_general | solution.py:119
  326.9 7.7 %all-to-all-done.1 = bf16[8,768,96]{1,2,0:T(8,128)(2,1)} async-done(((bf16[8,768,96]{1,2,0:T(8,128)(2,1)}), bf16[8,768,96]{1,2,0:T(8,128)(2,1)}, u32[]{:S(2)}, u32[]{:S(2)}) %all-to-all-start.1) | async-done | bytes 1179680 | tf_op jit(solution)/shard_map/all_to_all | solution.py:21
  334.6 4.3 all-to-all-start
  338.9 2.3 reshape.139
  341.9 4.8 copy.76
  346.8 0.8 dynamic_slice.13
  348.8 2.2 convert_reduce_fusion.4
  351.0 4.7 all-to-all-done
  355.7 2.2 convert_reduce_fusion.5
  357.9 10.7 %reduce-scatter.3.cloned.1.call-done = bf16[3136,192]{0,1:T(8,128)(2,1)} async-done(((bf16[3136,768]{0,1:T(8,128)(2,1)}), bf16[3136,192]{0,1:T(8,128)(2,1)}) %reduce-scatter.3.cloned.1.call-update) | async-done | bytes 1204240 | tf_op jit(solution)/shard_map/reduce_scatter | solution.py:49
  368.5 1.5 fusion.17
  370.1 5.7 reshape.138
  375.8 84.1 %reduce-scatter.5.cloned.1.call-done = bf16[3136,192]{0,1:T(8,128)(2,1)} async-done(((bf16[3136,768]{0,1:T(8,128)(2,1)}), bf16[3136,192]{0,1:T(8,128)(2,1)}) %reduce-scatter.5.cloned.1.call-update) | async-done | bytes 1204240 | tf_op jit(solution)/shard_map/reduce_scatter | solution.py:49
  459.8 1.6 multiply_reduce_fusion.5
  462.2 5.7 reshape.130
  467.9 4.8 multiply_reduce_fusion.1
  472.7 19.7 %all-reduce.3 = (f32[16,196]{1,0:T(8,128)}, f32[16,196]{1,0:T(8,128)}) all-reduce(f32[16,196]{1,0:T(8,128)S(1)} %get-tuple-element.18, f32[16,196]{1,0:T(8,128)} %reduce_sum.187), channel_id=1, replica_groups=mesh['dp'=8,'tp'=4] {'tp'}, use_global_device_ids=true, to_apply=%region_13.0 | all-reduce | flops 6272 | bytes 50176 | tf_op jit(solution)/shard_map/psum | solution.py:33
  493.1 8.6 %convert_reduce_fusion.3 = (f32[196]{0:T(256)}, f32[16,196,192]{1,2,0:T(8,128)S(1)}, bf16[16,196,192]{1,2,0:T(8,128)(2,1)}) fusion(f32[16,196,192]{1,2,0:T(8,128)} %copy.76, f32[16,196]{1,0:T(8,128)} %get-tuple-element.34, f32[16,196,192]{1,2,0:T(8,128)} %copy-done.3, f32[16,196]{1,0:T(8,128)S(1)} %get-tuple-element.47, ...), kind=kLoop, calls=%fused_computation.32 | loop fusion | flops 8429372 | bytes 13298192 | tf_op jit(solution)/shard_map/reduce_sum | solution.py:139
  501.7 6.2 convolution_bitcast_fusion
  507.9 4.5 convert_reduce_fusion.1
  512.4 1.6 convolution_bitcast_fusion.1
  514.4 3.8 fusion.14
  519.8 0.8 broadcast_multiply_fusion
  520.6 2.4 copy.73
  523.0 3.6 reshape.129
  526.6 2.1 reduce_sum.195
  528.8 16.1 %all-reduce.2 = (f32[16,196]{1,0:T(8,128)S(1)}, f32[16,196]{1,0:T(8,128)S(1)}) all-reduce(f32[16,196]{1,0:T(8,128)S(1)} %get-tuple-element.16, f32[16,196]{1,0:T(8,128)S(1)} %get-tuple-element.21), channel_id=1, replica_groups=mesh['dp'=8,'tp'=4] {'tp'}, use_global_device_ids=true, to_apply=%region_17.0 | all-reduce | flops 6272 | bytes 50176 | tf_op jit(solution)/shard_map/psum | solution.py:33
  544.9 5.3 add_convert_fusion
  550.2 3.1 copy.77
  553.3 2.3 reshape.131
  555.6 39.9 %all-reduce = (f32[2,768]{1,0:T(2,128)S(1)}, f32[384]{0:T(512)}, f32[196]{0:T(256)}, f32[3072]{0:T(1024)}, f32[768]{0:T(1024)}) all-reduce(f32[2,768]{1,0:T(2,128)S(1)} %broadcast_multiply_fusion.6, f32[384]{0:T(512)S(1)} %copy-done.19, f32[196]{0:T(256)S(1)} %copy-done.18, ...), channel_id=1, replica_groups=mesh['dp'=8,'tp'=4] {'dp','tp'}, use_global_device_ids=true, to_apply=%region_24.0 | all-reduce | flops 5956 | bytes 47648 | tf_op jit(solution)/shard_map/psum | solution.py:153
  595.5 79.3 %all-reduce.8.cloned.1.call-done = (f32[64,2,768]{2,0,1:T(8,128)}, f32[196,384]{1,0:T(8,128)}, f32[384,196]{0,1:T(8,128)}) async-done(((f32[64,2,768]{2,0,1:T(8,128)}, f32[196,384]{1,0:T(8,128)}, f32[384,196]{0,1:T(8,128)}), (f32[64,2,768]{2,0,1:T(8,128)}, f32[196,384]{1,0:T(8,128)}, f32[384,196]{0,1:T(8,128)})) %all-reduce.8.cloned.1.call-update) | async-done | bytes 995344 | tf_op jit(solution)/shard_map/psum | solution.py:153
  674.8 1.1 multiply_reduce_fusion.7
  676.5 1.1 multiply_reduce_fusion.6
  678.2 1.7 copy.97
  679.9 1.7 copy.98
  (106 shorter events, 7.8 us)
Async XLA Ops:
  7.2 68.8 %all-gather.7.cloned.1.call-start = ((), (), s32[]{:S(2)}) async-start(), calls=%async_computation.5 | async-start | bytes 1327104 | tf_op jit(solution)/shard_map/all_gather | solution.py:101
  8.9 151.5 %all-gather.5.cloned.1.call-start = ((), (), s32[]{:S(2)}) async-start(), calls=%async_computation.4 | async-start | bytes 6144000 | tf_op jit(solution)/shard_map/all_gather | solution.py:45
  12.3 24.2 %copy-start.15 = (f32[192]{0:T(256)S(1)}, f32[192]{0:T(256)}, u32[]{:S(2)}) copy-start(f32[192]{0:T(256)} %param.16) | copy-start | bytes 2308
  12.3 24.2 %copy-start.20 = (f32[192]{0:T(256)S(1)}, f32[192]{0:T(256)}, u32[]{:S(2)}) copy-start(f32[192]{0:T(256)} %param.17) | copy-start | bytes 2308
  15.6 24.6 %copy-start.10 = (f32[196,384]{1,0:T(8,128)S(1)}, f32[196,384]{1,0:T(8,128)}, u32[]{:S(2)}) copy-start(f32[196,384]{1,0:T(8,128)} %param.18) | copy-start | bytes 903172
  39.0 1.1 copy-start.6
  40.2 1.9 copy-start
  40.2 1.9 copy-start.24
  40.2 1.9 copy-start.26
  40.2 1.9 copy-start.28
  42.1 2.5 copy-start.9
  42.1 18.4 %copy-start.13 = (f32[192]{0:T(256)S(1)}, f32[192]{0:T(256)}, u32[]{:S(2)}) copy-start(f32[192]{0:T(256)} %param.22) | copy-start | bytes 2308
  44.6 19.2 %copy-start.3 = (f32[16,196,192]{1,2,0:T(8,128)}, f32[16,196,192]{1,2,0:T(8,128)S(1)}, u32[]{:S(2)}) copy-start(f32[16,196,192]{1,2,0:T(8,128)S(1)} %get-tuple-element.55) | copy-start | bytes 7225348
  68.1 117.2 %all-gather.9.cloned.1.call-start = ((), (), s32[]{:S(2)}) async-start(), calls=%async_computation.6 | async-start | bytes 1327104 | tf_op jit(solution)/shard_map/all_gather | solution.py:102
  69.8 209.6 %all-gather.11.cloned.1.call-start = ((), (), s32[]{:S(2)}) async-start(), calls=%async_computation.8 | async-start | bytes 6144000 | tf_op jit(solution)/shard_map/all_gather | solution.py:45
  74.9 293.6 %reduce-scatter.3.cloned.1.call-start = ((), (), s32[]{:S(2)}) async-start(), calls=%async_computation.7 | async-start | bytes 6144000 | tf_op jit(solution)/shard_map/reduce_scatter | solution.py:49
  196.0 100.9 %copy-start.23 = (bf16[768,768]{1,0:T(8,128)(2,1)S(1)}, bf16[768,768]{1,0:T(8,128)(2,1)}, u32[]{:S(2)}) copy-start(bf16[768,768]{1,0:T(8,128)(2,1)} %all-gather.7.cloned.1.call-done) | copy-start | bytes 3538948
  196.0 263.8 %reduce-scatter.5.cloned.1.call-start = ((), (), s32[]{:S(2)}) async-start(), calls=%async_computation.9 | async-start | bytes 6144000 | tf_op jit(solution)/shard_map/reduce_scatter | solution.py:49
  294.7 2.2 copy-start.29
  313.3 21.3 %all-to-all-start.1 = ((bf16[8,768,96]{1,2,0:T(8,128)(2,1)}), bf16[8,768,96]{1,2,0:T(8,128)(2,1)}, u32[]{:S(2)}, u32[]{:S(2)}) async-start(bf16[8,768,96]{1,2,0:T(8,128)(2,1)} %bitcast.18), calls=%async_computation.3 | async-start | bytes 2359296 | tf_op jit(solution)/shard_map/all_to_all | solution.py:21
  326.8 12.1 %copy-start.8 = (bf16[16,1,37632]{2,0,1:T(8,128)(2,1)S(1)}, bf16[16,1,37632]{2,0,1:T(8,128)(2,1)}, u32[]{:S(2)}) copy-start(bf16[16,1,37632]{2,0,1:T(8,128)(2,1)} %param.29) | copy-start | bytes 3612676
  334.6 21.1 %all-to-all-start = ((bf16[8,96,768]{2,1,0:T(8,128)(2,1)}), bf16[8,96,768]{2,1,0:T(8,128)(2,1)}, u32[]{:S(2)}, u32[]{:S(2)}) async-start(bf16[8,96,768]{2,1,0:T(8,128)(2,1)} %bitcast.81), calls=%async_computation.2 | async-start | bytes 2359296 | tf_op jit(solution)/shard_map/all_to_all | solution.py:21
  338.9 335.9 %all-reduce.8.cloned.1.call-start = ((), (), s32[]{:S(2)}) async-start(), calls=%async_computation.10 | async-start | bytes 2015232 | tf_op jit(solution)/shard_map/psum | solution.py:153
  370.0 89.8 %copy-start.14 = (f32[192]{0:T(256)S(1)}, f32[192]{0:T(256)}, u32[]{:S(2)}) copy-start(f32[192]{0:T(256)} %param.22) | copy-start | bytes 2308
  493.1 8.6 %copy-start.27 = (f32[384]{0:T(512)S(1)}, f32[384]{0:T(512)}, u32[]{:S(2)}) copy-start(f32[384]{0:T(512)} %param.19) | copy-start | bytes 4612
  493.1 14.8 %slice-start = ((s8[4718592]{0:T(1024)(128)(4,1)}), s8[4194304]{0:T(1024)(128)(4,1)S(1)}, s32[]{:S(2)}) async-start(s8[4718592]{0:T(1024)(128)(4,1)} %bitcast.79), calls=%async_computation.11 | async-start | bytes 8388608
  501.7 6.2 copy-start.4
  501.7 6.2 slice-start.1
  501.7 6.2 copy-start.25
  507.9 4.5 copy-start.7
  512.4 2.0 copy-start.1
  512.4 2.0 copy-start.16
  518.2 0.8 copy-start.22
  518.7 1.9 copy-start.5
  522.9 5.8 copy-start.21
  523.0 22.0 %copy-start.2 = (f32[16,196,192]{1,2,0:T(8,128)S(1)}, f32[16,196,192]{1,2,0:T(8,128)}, u32[]{:S(2)}) copy-start(f32[16,196,192]{1,2,0:T(8,128)} %copy.70) | copy-start | bytes 7225348
  523.0 22.0 %copy-start.17 = (f32[192]{0:T(256)S(1)}, f32[192]{0:T(256)}, u32[]{:S(2)}) copy-start(f32[192]{0:T(256)} %param.16) | copy-start | bytes 2308
  550.2 5.4 copy-start.11
  550.2 5.4 copy-start.12
  550.2 5.4 copy-start.18
  550.2 5.4 copy-start.19
Sparse Core Ops, SparseCore 0:
  10.5 26.7 all-gather.6
  68.2 92.0 all-gather.4
  162.8 22.4 all-gather.8
  186.8 92.6 all-gather.10
  281.6 86.8 reduce-scatter.2
  370.8 88.9 reduce-scatter.4
  545.0 129.7 all-reduce.7
where the time goes:
time: 698 us; the launch traced here: 689 us
  waiting for transfers between devices  369 us (53%)
  blocking collectives  112 us (16%)
  matrix products  81.5 us (12%)
  local copies, waits for them, and re-layouts  59.5 us (9%)
  other arithmetic  42.3 us (6%)
  between operations  15 us (2%)
  starting transfers between devices  9.6 us (1%)
    all_gather x2, waiting for transfers between devices, gather_channels(): return lax.all_gather(values, 'tp', axis=1, tiled=True)  167 us
    reduce_scatter x2, waiting for transfers between devices, sum_channels(): lax.psum_scatter(values.astype(jnp.bfloat16), 'tp', scatter_dimension=1,...  94.7 us
    psum x1, waiting for transfers between devices, per_device(): lax.psum((token_w1_grad, token_b1_grad, token_w2_grad, token_b2_grad, spr...  79.3 us
    psum x1, blocking collectives, per_device(): lax.psum((token_w1_grad, token_b1_grad, token_w2_grad, token_b2_grad, spr...  39.9 us
    psum x2, blocking collectives, norm_stats(): totals = lax.psum((jnp.sum(values, -1), jnp.sum(values * values, -1)), 'tp')  36.8 us
    psum x2, blocking collectives, norm_back(): lax.psum((jnp.sum(grad_hat, -1), jnp.sum(grad_hat * normed, -1)), 'tp')  35.7 us
    dot_general x1, matrix products, per_device(): jnp.dot(grad_full, lower_rows.T, preferred_element_type=f32)  15.2 us
    all_gather x1, waiting for transfers between devices, per_device(): lax.all_gather(ch_w2.astype(bf16), 'dp', axis=1, tiled=True)  14.6 us
  transfers between devices with their start and end apart: 9, of which 8 were waited for; matrix products, arithmetic and copies ran while one was open for 18% of the time, Pallas kernels for 0%

commit v1 on v0

--- a/solution.py
+++ b/solution.py
@@ -1,3 +1,4 @@
+import functools
 import math
 import jax
 import jax.numpy as jnp
@@ -8,6 +9,40 @@
 GROUPS = 64
 epsilon = 1e-06
 highest = lax.Precision.HIGHEST
+
+
+def turn_bands_on(field, axis_id):
+    piece_now, low, block_now = (lax.axis_size(axis_id), lax.axis_index(axis_id), field.shape[1])
+    leaves = []
+    no = 0
+    while no < piece_now:
+        leaves.append((no, (no + 1) % piece_now))
+        no = no + 1
+    parts_seen = []
+    no = 0
+    while no < piece_now:
+        parts_seen.append((no, (no - 1) % piece_now))
+        no += 1
+    response = jnp.zeros((*field.shape[:1], piece_now * block_now, *field.shape[2:]), field.dtype)
+    response = lax.dynamic_update_slice_in_dim(response, field, low * block_now, axis=1)
+    heard = piece_now // 2
+    idx = 1
+    r2 = x_new = field
+    while idx < heard + 1:
+        r2 = lax.ppermute(r2, perm=leaves, axis_name=axis_id)
+        response = lax.dynamic_update_slice_in_dim(
+            response, r2, (low - idx) % piece_now * block_now, axis=1
+        )
+        if idx < piece_now - heard:
+            x_new = lax.ppermute(x_new, axis_id, perm=parts_seen)
+            response = lax.dynamic_update_slice_in_dim(
+                response, x_new, (low + idx) % piece_now * block_now, axis=1
+            )
+        idx = idx + 1
+    return response
+
+
+_set_table = functools.partial(turn_bands_on, axis_id="dp")
 
 
 def in_blocks(array, dim, size):
@@ -99,7 +134,7 @@
     grad_low = plain_grad.reshape(row_count, local_width)
     upper_rows, lower_rows = (
         lax.all_gather(ch_w1.astype(bf16), "dp", axis=0, tiled=True),
-        lax.all_gather(ch_w2.astype(bf16), "dp", axis=1, tiled=True),
+        _set_table(ch_w2.astype(bf16)),
     )
     gathered = gather_channels(branch_in)
     hidden_width = upper_rows.shape[1]

time: 698 us -> 672 us (0.963)
  waiting for transfers between devices: 369 us -> 339 us
  starting transfers between devices: 9.6 us -> 17.5 us
  matrix products: 81.5 us -> 73.8 us
    all_gather x2, waiting for transfers between devices: 167 us -> 137 us  [gather_channels(): return lax.all_gather(values, 'tp', axis=1, tiled=True)]
    ppermute x0 -> x7, waiting for transfers between devices: none -> 14.6 us  [the longest x4 14.6 us: turn_bands_on(): r2 = lax.ppermute(r2, perm=leaves, axis_name=axis_id)]
    all_gather x1 -> x0, waiting for transfers between devices: 14.6 us -> none  [per_device(): lax.all_gather(ch_w2.astype(bf16), 'dp', axis=1, tiled=True)]
    ppermute x0 -> x7, starting transfers between devices: none -> 8.12 us  [the longest x3 7.91 us: turn_bands_on(): x_new = lax.ppermute(x_new, axis_id, perm=parts_seen)]
  transfers between devices with their start and end apart: 9 -> 15, of which waited for: 8 -> 11; matrix products, arithmetic and copies ran while one was open for 18% -> 17% of each run, Pallas kernels for 0% -> 0%
where the time goes in v1:
time: 672 us; the launch traced here: 663 us
  waiting for transfers between devices  339 us (50%)
  blocking collectives  112 us (17%)
  matrix products  73.8 us (11%)
  local copies, waits for them, and re-layouts  63.8 us (9%)
  other arithmetic  41.4 us (6%)
  starting transfers between devices  17.5 us (3%)
  between operations  15.1 us (2%)
    all_gather x2, waiting for transfers between devices, gather_channels(): return lax.all_gather(values, 'tp', axis=1, tiled=True)  137 us
    reduce_scatter x2, waiting for transfers between devices, sum_channels(): lax.psum_scatter(values.astype(jnp.bfloat16), 'tp', scatter_dimension=1,...  94.8 us
    psum x1, waiting for transfers between devices, per_device(): lax.psum((token_w1_grad, token_b1_grad, token_w2_grad, token_b2_grad, spr...  79.3 us
    psum x1, blocking collectives, per_device(): lax.psum((token_w1_grad, token_b1_grad, token_w2_grad, token_b2_grad, spr...  39.9 us
    psum x2, blocking collectives, norm_stats(): totals = lax.psum((jnp.sum(values, -1), jnp.sum(values * values, -1)), 'tp')  36.8 us
    psum x2, blocking collectives, norm_back(): lax.psum((jnp.sum(grad_hat, -1), jnp.sum(grad_hat * normed, -1)), 'tp')  35.7 us
    dot_general x1, matrix products, per_device(): jnp.dot(grad_full, lower_rows.T, preferred_element_type=f32)  15.2 us
    ppermute x4, waiting for transfers between devices, turn_bands_on(): r2 = lax.ppermute(r2, perm=leaves, axis_name=axis_id)  14.6 us
  transfers between devices with their start and end apart: 15, of which 11 were waited for; matrix products, arithmetic and copies ran while one was open for 17% of the time, Pallas kernels for 0%

profile of v1, /device:TPU:0, one launch (start us, length us, event | category | flops | bytes accessed | tf_op | source)
XLA Modules:
  0.0 662.5 jit_solution(5727268090882115338)
XLA Ops:
  7.2 1.6 convert_element_type.122
  8.9 2.2 reshape.136
  11.2 1.2 fusion.38
  12.3 3.2 copy.70
  15.6 20.9 %all-reduce.5 = (f32[16,196]{1,0:T(8,128)S(1)}, f32[16,196]{1,0:T(8,128)S(1)}) all-reduce(f32[16,196]{1,0:T(8,128)S(1)} %get-tuple-element.20, f32[16,196]{1,0:T(8,128)S(1)} %get-tuple-element.19), channel_id=1, replica_groups=mesh['dp'=8,'tp'=4] {'tp'}, use_global_device_ids=true, to_apply=%region_3.0 | all-reduce | flops 6272 | bytes 50176 | tf_op jit(solution)/shard_map/psum | solution.py:61
  36.5 2.5 add_convert_fusion.2
  39.0 1.1 copy-done.6
  42.1 2.5 fusion.39
  44.6 15.8 %all-reduce.4 = (f32[16,196]{1,0:T(8,128)S(1)}, f32[16,196]{1,0:T(8,128)S(1)}) all-reduce(f32[16,196]{1,0:T(8,128)S(1)} %get-tuple-element.23, f32[16,196]{1,0:T(8,128)S(1)} %get-tuple-element.22), channel_id=1, replica_groups=mesh['dp'=8,'tp'=4] {'tp'}, use_global_device_ids=true, to_apply=%region_7.0 | all-reduce | flops 6272 | bytes 50176 | tf_op jit(solution)/shard_map/psum | solution.py:61
  60.5 1.3 add_convert_fusion.1
  61.7 2.0 copy.71
  63.8 4.3 reshape.126
  68.2 3.1 reshape_reshape.3
  71.2 2.0 copy.74
  74.1 2.6 collective-permute-start.1
  77.5 2.3 collective-permute-done
  80.0 2.6 collective-permute-start.3
  82.7 3.2 collective-permute-done.2
  85.8 2.6 collective-permute-start.5
  88.5 3.7 collective-permute-done.4
  92.3 5.4 collective-permute-done.6
  97.8 62.6 %all-gather.4.cloned.1.call-done = bf16[3136,768]{0,1:T(8,128)(2,1)} async-done(((bf16[3136,192]{0,1:T(8,128)(2,1)}), bf16[3136,768]{0,1:T(8,128)(2,1)}) %all-gather.4.cloned.1.call-update) | async-done | bytes 4816912 | tf_op jit(solution)/shard_map/all_gather | solution.py:80
  160.4 6.7 %fusion.42 = f32[3136,768]{1,0:T(8,128)S(1)} fusion(bf16[3136,768]{0,1:T(8,128)(2,1)} %all-gather.4.cloned.1.call-done, bf16[768,768]{1,0:T(8,128)(2,1)} %all-gather.6.cloned.1.call-done), kind=kOutput, calls=%fused_computation.105 | convolution fusion | flops 3699376128 | bytes 15630336 | tf_op jit(solution)/shard_map/dot_general | solution.py:143
  167.1 4.1 copy-done.30
  171.2 6.6 convolution_convert_fusion.1
  178.2 74.8 %all-gather.8.cloned.1.call-done = bf16[3136,768]{0,1:T(8,128)(2,1)} async-done(((bf16[3136,192]{0,1:T(8,128)(2,1)}), bf16[3136,768]{0,1:T(8,128)(2,1)}) %all-gather.8.cloned.1.call-update) | async-done | bytes 4816912 | tf_op jit(solution)/shard_map/all_gather | solution.py:80
  253.1 15.2 %convert_reduce_fusion = (f32[768]{0:T(1024)S(1)}, bf16[3136,768]{1,0:T(8,128)(2,1)S(1)}) fusion(f32[3136,768]{1,0:T(8,128)} %copy-done.30, f32[768]{0:T(1024)S(1)} %dynamic_slice.12, bf16[768,768]{0,1:T(8,128)(2,1)S(1)} %constant_dynamic-update-slice_fusion, bf16[3136,768]{0,1:T(8,128)(2,1)} %all-gather.8.cloned.1.call-done), kind=kOutput, calls=%fused_computation.14 | convolution fusion | flops 3754769664 | bytes 20453376 | tf_op jit(solution)/shard_map/dot_general | solution.py:151
  268.3 2.1 copy-done.31
  270.4 5.8 convolution_convert_fusion
  276.3 10.6 %convolution_convert_fusion.2 = bf16[768,768]{0,1:T(8,128)(2,1)} fusion(bf16[3136,768]{0,1:T(8,128)(2,1)} %all-gather.8.cloned.1.call-done, f32[3136,768]{1,0:T(8,128)} %copy-done.30, f32[768]{0:T(1024)S(1)} %dynamic_slice.12), kind=kOutput, calls=%fused_computation.54 | convolution fusion | flops 3724050432 | bytes 15633408 | tf_op jit(solution)/shard_map/dot_general | solution.py:152
  286.9 4.4 all-to-all-start.1
  291.3 9.1 %convolution_convert_fusion.3 = bf16[768,768]{1,0:T(8,128)(2,1)} fusion(bf16[3136,768]{0,1:T(8,128)(2,1)} %all-gather.4.cloned.1.call-done, bf16[3136,768]{1,0:T(8,128)(2,1)} %copy-done.31), kind=kOutput, calls=%fused_computation.55 | convolution fusion | flops 3699965952 | bytes 10813440 | tf_op jit(solution)/shard_map/dot_general | solution.py:154
  300.4 7.7 %all-to-all-done.1 = bf16[8,768,96]{1,2,0:T(8,128)(2,1)} async-done(((bf16[8,768,96]{1,2,0:T(8,128)(2,1)}), bf16[8,768,96]{1,2,0:T(8,128)(2,1)}, u32[]{:S(2)}, u32[]{:S(2)}) %all-to-all-start.1) | async-done | bytes 1179680 | tf_op jit(solution)/shard_map/all_to_all | solution.py:56
  308.2 4.3 all-to-all-start
  312.5 2.3 reshape.139
  315.5 4.8 copy.76
  322.4 2.2 convert_reduce_fusion.4
  324.5 4.7 all-to-all-done
  329.2 2.2 convert_reduce_fusion.5
  331.4 10.7 %reduce-scatter.3.cloned.1.call-done = bf16[3136,192]{0,1:T(8,128)(2,1)} async-done(((bf16[3136,768]{0,1:T(8,128)(2,1)}), bf16[3136,192]{0,1:T(8,128)(2,1)}) %reduce-scatter.3.cloned.1.call-update) | async-done | bytes 1204240 | tf_op jit(solution)/shard_map/reduce_scatter | solution.py:84
  342.1 1.5 fusion.20
  343.7 5.7 reshape.138
  349.3 84.1 %reduce-scatter.5.cloned.1.call-done = bf16[3136,192]{0,1:T(8,128)(2,1)} async-done(((bf16[3136,768]{0,1:T(8,128)(2,1)}), bf16[3136,192]{0,1:T(8,128)(2,1)}) %reduce-scatter.5.cloned.1.call-update) | async-done | bytes 1204240 | tf_op jit(solution)/shard_map/reduce_scatter | solution.py:84
  433.4 1.6 multiply_reduce_fusion.5
  435.8 5.7 reshape.130
  441.5 4.8 multiply_reduce_fusion.1
  446.3 19.7 %all-reduce.3 = (f32[16,196]{1,0:T(8,128)}, f32[16,196]{1,0:T(8,128)}) all-reduce(f32[16,196]{1,0:T(8,128)S(1)} %get-tuple-element.18, f32[16,196]{1,0:T(8,128)} %reduce_sum.187), channel_id=1, replica_groups=mesh['dp'=8,'tp'=4] {'tp'}, use_global_device_ids=true, to_apply=%region_13.14 | all-reduce | flops 6272 | bytes 50176 | tf_op jit(solution)/shard_map/psum | solution.py:68
  466.7 8.6 %convert_reduce_fusion.3 = (f32[196]{0:T(256)}, f32[16,196,192]{1,2,0:T(8,128)S(1)}, bf16[16,196,192]{1,2,0:T(8,128)(2,1)}) fusion(f32[16,196,192]{1,2,0:T(8,128)} %copy.76, f32[16,196]{1,0:T(8,128)} %get-tuple-element.34, f32[16,196,192]{1,2,0:T(8,128)} %copy-done.3, f32[16,196]{1,0:T(8,128)S(1)} %get-tuple-element.47, ...), kind=kLoop, calls=%fused_computation.37 | loop fusion | flops 8429372 | bytes 13298192 | tf_op jit(solution)/shard_map/reduce_sum | solution.py:174
  475.3 6.2 convolution_bitcast_fusion
  481.5 4.5 convert_reduce_fusion.1
  486.0 1.6 convolution_bitcast_fusion.1
  488.0 3.8 fusion.17
  494.2 2.4 copy.73
  496.6 3.6 reshape.129
  500.2 2.1 reduce_sum.195
  502.5 16.1 %all-reduce.2 = (f32[16,196]{1,0:T(8,128)S(1)}, f32[16,196]{1,0:T(8,128)S(1)}) all-reduce(f32[16,196]{1,0:T(8,128)S(1)} %get-tuple-element.16, f32[16,196]{1,0:T(8,128)S(1)} %get-tuple-element.21), channel_id=1, replica_groups=mesh['dp'=8,'tp'=4] {'tp'}, use_global_device_ids=true, to_apply=%region_17.18 | all-reduce | flops 6272 | bytes 50176 | tf_op jit(solution)/shard_map/psum | solution.py:68
  518.6 5.3 add_convert_fusion
  523.9 3.1 copy.77
  526.9 2.3 reshape.131
  529.2 39.9 %all-reduce = (f32[2,768]{1,0:T(2,128)S(1)}, f32[384]{0:T(512)}, f32[196]{0:T(256)}, f32[3072]{0:T(1024)}, f32[768]{0:T(1024)}) all-reduce(f32[2,768]{1,0:T(2,128)S(1)} %broadcast_multiply_fusion.6, f32[384]{0:T(512)S(1)} %copy-done.20, f32[196]{0:T(256)S(1)} %copy-done.19, ...), channel_id=1, replica_groups=mesh['dp'=8,'tp'=4] {'dp','tp'}, use_global_device_ids=true, to_apply=%region_24.25 | all-reduce | flops 5956 | bytes 47648 | tf_op jit(solution)/shard_map/psum | solution.py:188
  569.1 79.3 %all-reduce.8.cloned.1.call-done = (f32[64,2,768]{2,0,1:T(8,128)}, f32[196,384]{1,0:T(8,128)}, f32[384,196]{0,1:T(8,128)}) async-done(((f32[64,2,768]{2,0,1:T(8,128)}, f32[196,384]{1,0:T(8,128)}, f32[384,196]{0,1:T(8,128)}), (f32[64,2,768]{2,0,1:T(8,128)}, f32[196,384]{1,0:T(8,128)}, f32[384,196]{0,1:T(8,128)})) %all-reduce.8.cloned.1.call-update) | async-done | bytes 995344 | tf_op jit(solution)/shard_map/psum | solution.py:188
  648.4 1.1 multiply_reduce_fusion.7
  651.9 1.7 copy.105
  653.6 1.7 copy.106
  (129 shorter events, 13.9 us)
Async XLA Ops:
  7.2 90.6 %all-gather.6.cloned.1.call-start = ((), (), s32[]{:S(2)}) async-start(), calls=%async_computation.5 | async-start | bytes 1327104 | tf_op jit(solution)/shard_map/all_gather | solution.py:136
  8.9 151.5 %all-gather.4.cloned.1.call-start = ((), (), s32[]{:S(2)}) async-start(), calls=%async_computation.4 | async-start | bytes 6144000 | tf_op jit(solution)/shard_map/all_gather | solution.py:80
  12.3 24.2 %copy-start.16 = (f32[192]{0:T(256)S(1)}, f32[192]{0:T(256)}, u32[]{:S(2)}) copy-start(f32[192]{0:T(256)} %param.16) | copy-start | bytes 2308
  12.3 24.2 %copy-start.21 = (f32[192]{0:T(256)S(1)}, f32[192]{0:T(256)}, u32[]{:S(2)}) copy-start(f32[192]{0:T(256)} %param.17) | copy-start | bytes 2308
  15.6 24.6 %copy-start.10 = (f32[196,384]{1,0:T(8,128)S(1)}, f32[196,384]{1,0:T(8,128)}, u32[]{:S(2)}) copy-start(f32[196,384]{1,0:T(8,128)} %param.18) | copy-start | bytes 903172
  39.0 1.1 copy-start.6
  40.2 1.9 copy-start
  40.2 1.9 copy-start.25
  40.2 1.9 copy-start.27
  40.2 1.9 copy-start.29
  42.1 2.5 copy-start.9
  42.1 18.4 %copy-start.14 = (f32[192]{0:T(256)S(1)}, f32[192]{0:T(256)}, u32[]{:S(2)}) copy-start(f32[192]{0:T(256)} %param.22) | copy-start | bytes 2308
  44.6 19.2 %copy-start.3 = (f32[16,196,192]{1,2,0:T(8,128)}, f32[16,196,192]{1,2,0:T(8,128)S(1)}, u32[]{:S(2)}) copy-start(f32[16,196,192]{1,2,0:T(8,128)S(1)} %get-tuple-element.55) | copy-start | bytes 7225348
  68.1 184.9 %all-gather.8.cloned.1.call-start = ((), (), s32[]{:S(2)}) async-start(), calls=%async_computation.7 | async-start | bytes 6144000 | tf_op jit(solution)/shard_map/all_gather | solution.py:80
  71.2 2.2 copy-start.11
  73.3 268.9 %reduce-scatter.3.cloned.1.call-start = ((), (), s32[]{:S(2)}) async-start(), calls=%async_computation.6 | async-start | bytes 6144000 | tf_op jit(solution)/shard_map/reduce_scatter | solution.py:84
  74.1 5.7 collective-permute-start
  74.1 5.9 collective-permute-start.1
  79.8 6.1 collective-permute-start.2
  80.0 5.9 collective-permute-start.3
  85.8 6.4 collective-permute-start.4
  85.8 6.4 collective-permute-start.5
  92.3 5.5 collective-permute-start.6
  167.1 4.1 copy-start.30
  177.8 255.6 %reduce-scatter.5.cloned.1.call-start = ((), (), s32[]{:S(2)}) async-start(), calls=%async_computation.8 | async-start | bytes 6144000 | tf_op jit(solution)/shard_map/reduce_scatter | solution.py:84
  253.1 17.4 %copy-start.24 = (bf16[768,768]{1,0:T(8,128)(2,1)S(1)}, bf16[768,768]{1,0:T(8,128)(2,1)}, u32[]{:S(2)}) copy-start(bf16[768,768]{1,0:T(8,128)(2,1)} %all-gather.6.cloned.1.call-done) | copy-start | bytes 3538948
  268.3 2.2 copy-start.31
  286.9 21.3 %all-to-all-start.1 = ((bf16[8,768,96]{1,2,0:T(8,128)(2,1)}), bf16[8,768,96]{1,2,0:T(8,128)(2,1)}, u32[]{:S(2)}, u32[]{:S(2)}) async-start(bf16[8,768,96]{1,2,0:T(8,128)(2,1)} %bitcast.19), calls=%async_computation.3 | async-start | bytes 2359296 | tf_op jit(solution)/shard_map/all_to_all | solution.py:56
  300.4 12.1 %copy-start.8 = (bf16[16,1,37632]{2,0,1:T(8,128)(2,1)S(1)}, bf16[16,1,37632]{2,0,1:T(8,128)(2,1)}, u32[]{:S(2)}) copy-start(bf16[16,1,37632]{2,0,1:T(8,128)(2,1)} %param.29) | copy-start | bytes 3612676
  308.2 21.1 %all-to-all-start = ((bf16[8,96,768]{2,1,0:T(8,128)(2,1)}), bf16[8,96,768]{2,1,0:T(8,128)(2,1)}, u32[]{:S(2)}, u32[]{:S(2)}) async-start(bf16[8,96,768]{2,1,0:T(8,128)(2,1)} %bitcast.94), calls=%async_computation.2 | async-start | bytes 2359296 | tf_op jit(solution)/shard_map/all_to_all | solution.py:56
  312.4 336.0 %all-reduce.8.cloned.1.call-start = ((), (), s32[]{:S(2)}) async-start(), calls=%async_computation.9 | async-start | bytes 2015232 | tf_op jit(solution)/shard_map/psum | solution.py:188
  343.6 89.8 %copy-start.15 = (f32[192]{0:T(256)S(1)}, f32[192]{0:T(256)}, u32[]{:S(2)}) copy-start(f32[192]{0:T(256)} %param.22) | copy-start | bytes 2308
  466.7 8.6 %copy-start.28 = (f32[384]{0:T(512)S(1)}, f32[384]{0:T(512)}, u32[]{:S(2)}) copy-start(f32[384]{0:T(512)} %param.19) | copy-start | bytes 4612
  466.7 14.8 %slice-start = ((s8[4718592]{0:T(1024)(128)(4,1)}), s8[4194304]{0:T(1024)(128)(4,1)S(1)}, s32[]{:S(2)}) async-start(s8[4718592]{0:T(1024)(128)(4,1)} %bitcast.92), calls=%async_computation.10 | async-start | bytes 8388608
  475.3 6.2 copy-start.4
  475.3 6.2 slice-start.1
  475.3 6.2 copy-start.26
  481.5 4.5 copy-start.7
  486.0 2.0 copy-start.1
  486.0 2.0 copy-start.17
  491.8 0.8 copy-start.23
  492.3 1.9 copy-start.5
  496.6 5.8 copy-start.22
  496.6 22.0 %copy-start.2 = (f32[16,196,192]{1,2,0:T(8,128)S(1)}, f32[16,196,192]{1,2,0:T(8,128)}, u32[]{:S(2)}) copy-start(f32[16,196,192]{1,2,0:T(8,128)} %copy.70) | copy-start | bytes 7225348
  496.6 22.0 %copy-start.18 = (f32[192]{0:T(256)S(1)}, f32[192]{0:T(256)}, u32[]{:S(2)}) copy-start(f32[192]{0:T(256)} %param.16) | copy-start | bytes 2308
  523.9 5.4 copy-start.12
  523.9 5.4 copy-start.13
  523.9 5.4 copy-start.19
  523.9 5.4 copy-start.20
Sparse Core Ops, SparseCore 0:
  10.5 26.7 all-gather.5
  68.2 92.0 all-gather.3
  161.9 91.0 all-gather.7
  255.2 86.8 reduce-scatter.2
  344.4 88.9 reduce-scatter.4
  518.7 129.7 all-reduce.7
